TPU v7x, 32 devices: a whole 2x2x4 slice. The times are simulated.
32 devices in a mesh: grp: 4 (over y, core), ch: 8 (over z, x).
Axes of the slice: x: 2, y: 2, z: 4, core: 2. Of those that a mesh axis runs over, the one named last changes fastest.
Arguments:
- strain: bfloat16 [8, 1024, 4096], P('grp', 'ch'), may hold values from -6 to 6
- valid_mask: int32 [8, 1024], P('grp', 'ch'), may hold values 0 or 1
- pair_list: int32 [8, 6, 2], P('ch'), may hold values from 0 to 7, as said below
- owner_group: int32 [8, 6], P('ch'), may hold values from 0 to 3, as said below
Outputs:
- stacks: float32 [4, 8, 2, 128, 4096], P('grp', 'ch')
Inputs may be any that keep to these rules, and one draw needn't show every extreme that they name: `pair_list`: entries are channel block numbers; each ordered pair of blocks appears at most once over all columns. `owner_group`: in each column no group owns more than 2 entries, and some group owns exactly 2.
All inputs are finite; a program needn't handle non-finite values. No bound on the sum of `valid_mask` on one device may be relied on, other than what follows from the above.
Results may differ from a plain program's by a relative error of at most 0.0042.
Values may be sent and summed in bfloat16 or wider, within the bound.
A program may use at most 192 MiB of HBM per device.

v0:
```python
import math

import jax
import jax.numpy as jnp
from jax import lax
from jax.sharding import PartitionSpec as P

NFFT = 4096
NB = 1024
SUB = 64
BLK = 128
CAP = 2


def forward_table(length, bins):
    samples = jnp.arange(length, dtype=jnp.int32)
    frequency = jnp.arange(1, bins + 1, dtype=jnp.int32)
    angles = jnp.mod(samples[:, None] * frequency[None, :], length).astype(jnp.float32) * (
        2.0 * math.pi / length
    )
    hann_taper = 0.5 - 0.5 * jnp.cos(samples.astype(jnp.float32) * (2.0 * math.pi / length))
    return jnp.concatenate(
        [hann_taper[:, None] * jnp.cos(angles), -hann_taper[:, None] * jnp.sin(angles)], axis=1
    ).astype(jnp.bfloat16)


def inverse_table(length, bins):
    frequency = jnp.arange(1, bins + 1, dtype=jnp.int32)
    lag_index = jnp.arange(length, dtype=jnp.int32) - length // 2
    angles = jnp.mod(frequency[:, None] * lag_index[None, :], length).astype(jnp.float32) * (
        2.0 * math.pi / length
    )
    return jnp.concatenate([jnp.cos(angles), -jnp.sin(angles)], axis=0)


def whiten_rows(spectrum, valid_mask, bins, band):
    real_part = spectrum[..., :bins]
    imag_part = spectrum[..., bins:]
    power = real_part * real_part + imag_part * imag_part
    band_power = jnp.sum(power.reshape(power.shape[:-1] + (bins // band, band)), axis=-1) / band
    norm_full = jnp.repeat(jnp.sqrt(band_power + 1e-06), band, axis=-1)
    norm_both = jnp.concatenate([norm_full, norm_full], axis=-1)
    return (spectrum / norm_both * valid_mask[..., None].astype(jnp.float32)).astype(jnp.bfloat16)


def cross_block(rows, pair_entry, block, bins):
    first_rows = lax.dynamic_slice_in_dim(rows, pair_entry[0] * block, block, 1).astype(jnp.float32)
    second_rows = lax.dynamic_slice_in_dim(rows, pair_entry[1] * block, block, 1).astype(
        jnp.float32
    )
    first_real = first_rows[..., :bins]
    first_imag = first_rows[..., bins:]
    second_real = second_rows[..., :bins]
    second_imag = second_rows[..., bins:]
    cross_real = jnp.sum(first_real * second_real + first_imag * second_imag, axis=0)
    cross_imag = jnp.sum(first_real * second_imag - first_imag * second_real, axis=0)
    return jnp.concatenate([cross_real, cross_imag], axis=-1)


def local(strain, valid_mask, pair_list, owner_group):
    window_count = strain.shape[0]
    groups = lax.axis_size("grp")
    forward = forward_table(NFFT, NB)
    spectrum = jnp.dot(strain.reshape(-1, NFFT), forward, preferred_element_type=jnp.float32)
    spectrum = spectrum.reshape(strain.shape[0], strain.shape[1], 2 * NB)
    white = whiten_rows(spectrum, valid_mask, NB, SUB)
    gathered = lax.all_gather(white, "ch", axis=1, tiled=True)
    pair_codes = pair_list[0]
    partial_value = lax.map(
        lambda pair_entry: cross_block(gathered, pair_entry, BLK, NB), pair_codes
    )
    owners = owner_group[0]
    list_len = owners.shape[0]
    positions = jnp.arange(list_len, dtype=jnp.int32)
    earlier = positions[None, :] < positions[:, None]
    slot_rank = jnp.sum(((owners[:, None] == owners[None, :]) & earlier).astype(jnp.int32), axis=1)
    slot_ids = jnp.arange(CAP, dtype=jnp.int32)
    flat_partial = partial_value.reshape(list_len, -1)
    summed = lax.psum(flat_partial, "grp")
    my_group = lax.axis_index("grp")
    picking = ((owners[None, :] == my_group) & (slot_rank[None, :] == slot_ids[:, None])).astype(
        jnp.float32
    )
    total = jnp.dot(
        picking, summed, precision=lax.Precision.HIGHEST, preferred_element_type=jnp.float32
    )
    inverse = inverse_table(NFFT, NB)
    stacked = jnp.dot(
        total.reshape(-1, 2 * NB),
        inverse,
        precision=lax.Precision.HIGHEST,
        preferred_element_type=jnp.float32,
    )
    scale = 1.0 / math.sqrt(NB * window_count * groups)
    return (stacked * scale).reshape(1, 1, CAP, BLK, NFFT)


def solution(mesh):
    placed = (P("grp", "ch", None), P("grp", "ch"), P("ch", None, None), P("ch", None))
    return jax.shard_map(
        local,
        mesh=mesh,
        in_specs=placed,
        out_specs=P("grp", "ch", None, None, None),
        check_vma=False,
    )
```

profile of v0, /device:TPU:0, one launch (start us, length us, event | category | flops | bytes accessed | tf_op | source)
XLA Modules:
  0.0 475.3 jit_solution(4424673960620839761)
XLA Ops:
  6.6 0.8 convert_element_type.43
  7.4 69.9 %multiply_convert_fusion.1 = (bf16[4096,1024]{1,0:T(8,128)(2,1)}, bf16[4096,1024]{1,0:T(8,128)(2,1)}) fusion(s32[1024]{0:T(1024)S(1)} %iota_add_fusion.1, f32[4096]{0:T(1024)S(1)} %get-tuple-element.54, f32[4096]{0:T(1024)S(1)} %get-tuple-element.55), kind=kLoop, calls=%fused_computation.31 | loop fusion | flops 75497472 | bytes 16814080 | tf_op jit(solution)/shard_map/convert
  77.4 9.8 %fusion.11 = f32[2048,256]{0,1:T(8,128)} fusion(bf16[256,4096]{1,0:T(8,128)(2,1)S(1)} %bitcast.29, bf16[4096,1024]{1,0:T(8,128)(2,1)} %get-tuple-element.53, bf16[4096,1024]{1,0:T(8,128)(2,1)} %get-tuple-element.52), kind=kOutput, calls=%fused_computation.25 | convolution fusion | flops 4328521728 | bytes 20971520 | tf_op jit(solution)/shard_map/dot_general | solution.py:64
  87.2 1.9 copy.11
  89.5 1.2 fusion.23
  91.0 127.6 %all-gather.2.cloned.1.call-done = bf16[2,1024,2048]{1,2,0:T(8,128)(2,1)} async-done(((bf16[2,128,2048]{1,2,0:T(8,128)(2,1)}), bf16[2,1024,2048]{1,2,0:T(8,128)(2,1)}) %all-gather.2.cloned.1.call-update) | async-done | bytes 8388624 | tf_op jit(solution)/shard_map/all_gather | solution.py:67
  218.5 11.7 %copy.12 = bf16[2,1024,2048]{2,1,0:T(8,128)(2,1)} copy(bf16[2,1024,2048]{1,2,0:T(8,128)(2,1)} %all-gather.2.cloned.1.call-done) | data formatting | bytes 16777216 | tf_op jit(solution)/shard_map/while | solution.py:69
  230.2 32.5 %while.10 = (s32[]{:T(128)}, f32[6,128,2048]{2,1,0:T(8,128)}, s32[6,2]{0,1:T(2,128)S(1)}, bf16[2,1024,2048]{2,1,0:T(8,128)(2,1)}, s32[]{:T(128)}, /*index=5*/s32[1,1]{0,1:T(1,128)}, s32[]{:T(128)}, s32[]{:T(128)}) while((s32[]{:T(128)}, f32[6,128,2048]{2,1,0:T(8,128)}, s32[6,2]{0,1:T(2,128)S(1)}, bf16[2,1024,2048]{2,1,0:T(8,128)(2,1)}, ...), condition=%wide.region_5.6_spmd, body=%wide.region_2.0_spmd.sunk | while | flops 3145738 | bytes 13631721 | solution.py:69
  232.1 1.9 dynamic-slice_convert_fusion.3
  234.0 0.6 add_reduce_fusion.2
  234.6 1.1 fusion.42
  237.5 1.9 dynamic-slice_convert_fusion.3
  239.4 0.6 add_reduce_fusion.2
  240.0 1.1 fusion.42
  242.9 1.9 dynamic-slice_convert_fusion.3
  244.8 0.6 add_reduce_fusion.2
  245.4 1.1 fusion.42
  248.4 1.9 dynamic-slice_convert_fusion.3
  250.3 0.6 add_reduce_fusion.2
  250.8 1.1 fusion.42
  253.8 1.9 dynamic-slice_convert_fusion.3
  255.7 0.6 add_reduce_fusion.2
  256.2 1.1 fusion.42
  259.2 1.9 dynamic-slice_convert_fusion.3
  261.0 0.6 add_reduce_fusion.2
  261.6 1.1 fusion.42
  262.7 9.8 %copy.13 = f32[1,6,128,2048]{3,1,2,0:T(8,128)} copy(f32[1,6,128,2048]{3,2,1,0:T(8,128)} %bitcast.31) | data formatting | bytes 12582912
  272.7 68.4 %fusion.18 = (f32[1024,4096]{1,0:T(8,128)}, f32[1024,4096]{1,0:T(8,128)}) fusion(s32[4096]{0:T(1024)S(1)} %iota_add_fusion, s32[1024]{0:T(1024)S(1)} %iota_add_fusion.1), kind=kLoop, calls=%fused_computation.35 | loop fusion | flops 62914560 | bytes 33574912 | tf_op jit(solution)/shard_map/cos | solution.py:33
  341.2 82.5 %all-reduce.2.cloned.1.call-done = f32[6,262144]{1,0:T(8,128)} async-done(((f32[6,262144]{1,0:T(8,128)}), f32[6,262144]{1,0:T(8,128)}) %all-reduce.2.cloned.1.call-update) | async-done | bytes 6291472 | tf_op jit(solution)/shard_map/psum | solution.py:79
  423.7 7.4 %fusion.27 = f32[2,262144]{1,0:T(2,128)S(1)} fusion(f32[6,262144]{1,0:T(8,128)} %all-reduce.2.cloned.1.call-done, pred[6]{0:T(512)(128)(4,1)S(1)} %compare_bitcast_fusion, s32[6]{0:T(128)S(1)} %convert_reduce_fusion), kind=kOutput, calls=%fused_computation.52 | convolution fusion | flops 37748760 | bytes 8388638 | tf_op jit(solution)/shard_map/dot_general | solution.py:84
  431.1 3.1 reshape.62
  434.2 34.3 %fusion.19 = f32[256,4096]{1,0:T(8,128)} fusion(f32[256,2048]{1,0:T(8,128)} %reshape.62, f32[1024,4096]{1,0:T(8,128)} %get-tuple-element.51, f32[1024,4096]{1,0:T(8,128)} %get-tuple-element.50), kind=kOutput, calls=%fused_computation.36 | convolution fusion | flops 25779240960 | bytes 39845888 | tf_op jit(solution)/shard_map/dot_general | solution.py:88
  (33 shorter events, 4.5 us)
Async XLA Ops:
  6.5 70.9 %copy-start = (bf16[2,128,4096]{2,1,0:T(8,128)(2,1)S(1)}, bf16[2,128,4096]{2,1,0:T(8,128)(2,1)}, u32[]{:S(2)}) copy-start(bf16[2,128,4096]{2,1,0:T(8,128)(2,1)} %param.6) | copy-start | bytes 6291460
  6.5 212.0 %all-gather.2.cloned.1.call-start = ((), (), s32[]{:S(2)}) async-start(), calls=%async_computation | async-start | bytes 9437184 | tf_op jit(solution)/shard_map/all_gather | solution.py:67
  90.7 333.0 %all-reduce.2.cloned.1.call-start = ((), (), s32[]{:S(2)}) async-start(), calls=%async_computation.1 | async-start | bytes 16777216 | tf_op jit(solution)/shard_map/psum | solution.py:79
  91.0 139.3 %copy-start.2 = (s32[1,6,2]{1,2,0:T(2,128)S(1)}, s32[1,6,2]{1,2,0:T(2,128)}, u32[]{:S(2)}) copy-start(s32[1,6,2]{1,2,0:T(2,128)} %param.8) | copy-start | bytes 148
  262.7 9.8 %copy-start.3 = (s32[1,6]{1,0:T(1,128)S(1)}, s32[1,6]{1,0:T(1,128)}, u32[]{:S(2)}) copy-start(s32[1,6]{1,0:T(1,128)} %param.9) | copy-start | bytes 76
  434.2 34.3 %copy-start.1 = (bf16[2,128,4096]{2,1,0:T(8,128)(2,1)S(1)}, bf16[2,128,4096]{2,1,0:T(8,128)(2,1)}, u32[]{:S(2)}) copy-start(bf16[2,128,4096]{2,1,0:T(8,128)(2,1)} %param.6) | copy-start | bytes 6291460
Sparse Core Ops, SparseCore 0:
  90.9 127.6 all-gather.1
  272.6 151.0 all-reduce.1
where the time goes:
time: 476 us; the launch traced here: 475 us
  waiting for transfers between devices  210 us (44%)
  other arithmetic  162 us (34%)
  matrix products  51.5 us (11%)
  local copies, waits for them, and re-layouts  30.2 us (6%)
  between operations  13.5 us (3%)
  loops' own time  7.78 us (2%)
    all_gather x1, waiting for transfers between devices, local(): gathered = lax.all_gather(white, 'ch', axis=1, tiled=True)  128 us
    psum x1, waiting for transfers between devices, local(): summed = lax.psum(flat_partial, 'grp')  82.5 us
    another operation x1, other arithmetic  69.9 us
    cos x1, other arithmetic, inverse_table(): return jnp.concatenate([jnp.cos(angles), -jnp.sin(angles)], axis=0)  68.4 us
    dot_general x1, matrix products, local(): jnp.dot(total.reshape(-1, 2 * NB), inverse, precision=lax.Precision.HIGHE...  34.3 us
    while x1, local copies, waits for them, and re-layouts, local(): lax.map(lambda pair_entry: cross_block(gathered, pair_entry, BLK, NB), pa...  11.7 us
    convert_element_type x6, other arithmetic, cross_block(): lax.dynamic_slice_in_dim(rows, pair_entry[0] * block, block, 1)  11.3 us
    dot_general x1, matrix products, local(): jnp.dot(strain.reshape(-1, NFFT), forward, preferred_element_type=jnp.flo...  9.8 us
  transfers between devices with their start and end apart: 2, of which 2 were waited for; matrix products, arithmetic and copies ran while one was open for 14% of the time, Pallas kernels for 0%

commit v1 on v0

v1 whole, which is shorter than its diff:
```python
import functools
import math

import jax
import jax.numpy as jnp
import numpy as np
from jax import lax
from jax.experimental import pallas as pl
from jax.experimental.pallas import tpu as pltpu
from jax.sharding import PartitionSpec as P

NFFT = 4096
NB = 1024
SUB = 64
BLK = 128
CAP = 2
LANES = 128
MESH = pl.DeviceIdType.MESH


def row_bins(devices):
    bins = (np.arange(NB, dtype=np.int64) + 1).reshape(devices, 1, NB // devices)
    return np.broadcast_to(bins, (devices, 2, NB // devices)).reshape(-1)


def table_rows(devices, samples, taper):
    angles = np.mod(row_bins(devices)[:, None] * samples[None, :], NFFT) * (2.0 * math.pi / NFFT)
    is_imag = np.broadcast_to(
        np.array([False, True]).reshape(1, 2, 1), (devices, 2, NB // devices)
    ).reshape(-1, 1)
    return (np.where(is_imag, -np.sin(angles), np.cos(angles)) * taper[None, :]).astype(jnp.bfloat16)


@functools.lru_cache(maxsize=None)
def forward_rows(devices):
    samples = np.arange(NFFT, dtype=np.int64)
    taper = 0.5 - 0.5 * np.cos(samples * (2.0 * math.pi / NFFT))
    return table_rows(devices, samples, taper)


@functools.lru_cache(maxsize=None)
def inverse_rows(devices):
    return table_rows(devices, np.arange(NFFT, dtype=np.int64) - NFFT // 2, np.ones(NFFT))


def greet_all(groups, columns, me):
    devices = groups * columns
    barrier = pltpu.get_barrier_semaphore()

    def greet(step, carry):
        to = lax.rem(me + step, devices)
        pl.semaphore_signal(
            barrier,
            inc=1,
            device_id=(lax.div(to, columns), lax.rem(to, columns)),
            device_id_type=MESH,
        )
        return carry

    lax.fori_loop(1, devices, greet, 0)
    pl.semaphore_wait(barrier, devices - 1)


def block_copy(groups, columns, me, step, x_ref, y_ref, send_sem, recv_sem):
    to = lax.rem(me + step, groups * columns)
    return pltpu.make_async_remote_copy(
        src_ref=x_ref.at[to],
        dst_ref=y_ref.at[me],
        send_sem=send_sem.at[step],
        recv_sem=recv_sem.at[step],
        device_id=(lax.div(to, columns), lax.rem(to, columns)),
        device_id_type=MESH,
    )


def list_copy(columns, mine, step, list_ref, lists_ref, send_sem, recv_sem):
    return pltpu.make_async_remote_copy(
        src_ref=list_ref,
        dst_ref=lists_ref.at[mine],
        send_sem=send_sem.at[step],
        recv_sem=recv_sem.at[step],
        device_id=(lax.axis_index("grp"), lax.rem(mine + step, columns)),
        device_id_type=MESH,
    )


def loop(low, high, body):
    def step_body(step, carry):
        body(step)
        return carry

    lax.fori_loop(low, high, step_body, 0)


def exchange_kernel(groups, columns, with_lists, *refs):
    if with_lists:
        x_ref, list_ref, y_ref, lists_ref, own_sem, send_sem, recv_sem, lsend_sem, lrecv_sem = refs
    else:
        x_ref, y_ref, own_sem, send_sem, recv_sem = refs
    devices = groups * columns
    mine = lax.axis_index("ch")
    me = lax.axis_index("grp") * columns + mine
    greet_all(groups, columns, me)

    def copy_of(step):
        return block_copy(groups, columns, me, step, x_ref, y_ref, send_sem, recv_sem)

    def list_of(step):
        return list_copy(columns, mine, step, list_ref, lists_ref, lsend_sem, lrecv_sem)

    if with_lists:
        loop(1, columns, lambda step: list_of(step).start())
    loop(1, devices, lambda step: copy_of(step).start())
    own = pltpu.make_async_copy(x_ref.at[me], y_ref.at[me], own_sem.at[0])
    own.start()
    own.wait()
    if with_lists:
        own_list = pltpu.make_async_copy(list_ref, lists_ref.at[mine], own_sem.at[1])
        own_list.start()
        own_list.wait()
        loop(1, columns, lambda step: list_of(step).wait())
    loop(1, devices, lambda step: copy_of(step).wait())


def exchange(x, groups, columns, collective_id, own_list=None):
    devices = groups * columns
    with_lists = own_list is not None
    vmem = pl.BlockSpec(memory_space=pltpu.VMEM)
    out_shape = [jax.ShapeDtypeStruct(x.shape, x.dtype)]
    scratch = [
        pltpu.SemaphoreType.DMA((2,)),
        pltpu.SemaphoreType.DMA((devices,)),
        pltpu.SemaphoreType.DMA((devices,)),
    ]
    operands = [x]
    if with_lists:
        operands.append(own_list)
        out_shape.append(jax.ShapeDtypeStruct((columns,) + own_list.shape, own_list.dtype))
        scratch += [pltpu.SemaphoreType.DMA((columns,)), pltpu.SemaphoreType.DMA((columns,))]
    out = pl.pallas_call(
        functools.partial(exchange_kernel, groups, columns, with_lists),
        out_shape=out_shape,
        in_specs=[vmem] * len(operands),
        out_specs=[vmem] * len(out_shape),
        scratch_shapes=scratch,
        compiler_params=pltpu.CompilerParams(collective_id=collective_id, has_side_effects=True),
    )(*operands)
    return out if with_lists else out[0]


def cross_kernel(groups, columns, entries, scale, lists_ref, rows_ref, out_ref):
    half = rows_ref.shape[1] // 2
    windows = rows_ref.shape[2] // BLK
    out_ref[...] = jnp.zeros_like(out_ref)

    def column_body(column):
        for entry in range(entries):
            first = lists_ref[column, 2 * entry]
            second = lists_ref[column, 2 * entry + 1]
            owner = lists_ref[column, 2 * entries + entry]
            rank = jnp.int32(0)
            for before in range(entry):
                rank += (lists_ref[column, 2 * entries + before] == owner).astype(jnp.int32)
            real = jnp.zeros((half, BLK), jnp.float32)
            imag = jnp.zeros((half, BLK), jnp.float32)
            for group in range(groups):
                a = rows_ref[group * columns + first].astype(jnp.float32)
                b = rows_ref[group * columns + second].astype(jnp.float32)
                for window in range(windows):
                    lanes = slice(window * BLK, (window + 1) * BLK)
                    a_real, a_imag = a[:half, lanes], a[half:, lanes]
                    b_real, b_imag = b[:half, lanes], b[half:, lanes]
                    real += a_real * b_real + a_imag * b_imag
                    imag += a_real * b_imag - a_imag * b_real
            both = jnp.concatenate([real, imag], axis=0) * scale
            out_ref[owner * columns + column, rank] = both.astype(out_ref.dtype)

    loop(0, columns, column_body)


def local(strain, valid_mask, pair_list, owner_group):
    windows, channels = valid_mask.shape
    groups = lax.axis_size("grp")
    columns = lax.axis_size("ch")
    devices = groups * columns
    entries = owner_group.shape[1]
    rows = 2 * NB // devices

    forward = jnp.asarray(forward_rows(devices))
    spectrum = lax.dot_general(
        forward,
        strain.reshape(windows * channels, NFFT),
        (((1,), (1,)), ((), ())),
        preferred_element_type=jnp.float32,
    ).reshape(devices, 2, rows // 2, windows * channels)
    power = jnp.sum(spectrum * spectrum, axis=1)
    band_power = jnp.sum(power.reshape(NB // SUB, SUB, -1), axis=1) / SUB
    gain = valid_mask.reshape(1, -1).astype(jnp.float32) / jnp.sqrt(band_power + 1e-06)
    gain = jnp.repeat(gain, SUB, axis=0).reshape(devices, 1, rows // 2, windows * channels)
    white = (spectrum * gain).astype(jnp.bfloat16).reshape(devices, rows, windows * channels)

    flat = jnp.concatenate([pair_list.reshape(-1), owner_group.reshape(-1)])
    own_list = jnp.broadcast_to(jnp.pad(flat, (0, LANES - flat.shape[0])), (8, LANES))
    gathered, lists = exchange(white, groups, columns, 0, own_list)

    scale = 1.0 / math.sqrt(NB * windows * groups)
    vmem = pl.BlockSpec(memory_space=pltpu.VMEM)
    slots = pl.pallas_call(
        functools.partial(cross_kernel, groups, columns, entries, scale),
        out_shape=jax.ShapeDtypeStruct((devices, CAP, rows, BLK), jnp.bfloat16),
        in_specs=[pl.BlockSpec(memory_space=pltpu.SMEM), vmem],
        out_specs=vmem,
    )(lists[:, 0, : 3 * entries], gathered)

    stack = exchange(slots, groups, columns, 1)
    stack = stack.transpose(1, 0, 2, 3).reshape(CAP, 2 * NB, BLK)
    stacked = jnp.einsum(
        "skr,kt->srt",
        stack,
        jnp.asarray(inverse_rows(devices)),
        preferred_element_type=jnp.float32,
    )
    return stacked.reshape(1, 1, CAP, BLK, NFFT)


def solution(mesh):
    placed = (P("grp", "ch", None), P("grp", "ch"), P("ch", None, None), P("ch", None))
    return jax.shard_map(
        local,
        mesh=mesh,
        in_specs=placed,
        out_specs=P("grp", "ch", None, None, None),
        check_vma=False,
    )
```

time: 476 us -> 99.2 us (0.21)
  waiting for transfers between devices: 210 us -> 0 us
  other arithmetic: 162 us -> 4.38 us
  Pallas kernels: 0 us -> 68.7 us
  matrix products: 51.5 us -> 19.9 us
  local copies, waits for them, and re-layouts: 30.2 us -> 5.75 us
  between operations: 13.5 us -> 0.07 us
  loops' own time: 7.78 us -> 0 us
    all_gather x1 -> x0, waiting for transfers between devices: 128 us -> none  [local(): gathered = lax.all_gather(white, 'ch', axis=1, tiled=True)]
    psum x1 -> x0, waiting for transfers between devices: 82.5 us -> none  [local(): summed = lax.psum(flat_partial, 'grp')]
    another operation x1 -> x0, other arithmetic: 69.9 us -> none
    pallas_call x0 -> x3, Pallas kernels: none -> 68.7 us  [the longest x2 63 us: exchange(): pl.pallas_call(functools.partial(exchange_kernel, groups, columns, with_l...]
    cos x1 -> x0, other arithmetic: 68.4 us -> none  [inverse_table(): return jnp.concatenate([jnp.cos(angles), -jnp.sin(angles)], axis=0)]
    dot_general x3 -> x2, matrix products: 51.5 us -> 19.9 us  [the longest x1 10.2 us: local(): jnp.einsum('skr,kt->srt', stack, jnp.asarray(inverse_rows(devices)), pref...]
    while x1 -> x0, local copies, waits for them, and re-layouts: 11.7 us -> none  [local(): lax.map(lambda pair_entry: cross_block(gathered, pair_entry, BLK, NB), pa...]
    convert_element_type x8 -> x2, other arithmetic: 13.3 us -> 3.6 us  [the longest x1 2.92 us: local(): (spectrum * gain).astype(jnp.bfloat16)]
  transfers between devices with their start and end apart: 2 -> 0, of which waited for: 2 -> 0; matrix products, arithmetic and copies ran while one was open for 14% -> 0% of each run, Pallas kernels for 0% -> 0%
where the time goes in v1:
time: 99.2 us; the launch traced here: 98.8 us
  Pallas kernels  68.7 us (69%)
  matrix products  19.9 us (20%)
  local copies, waits for them, and re-layouts  5.75 us (6%)
  other arithmetic  4.38 us (4%)
    pallas_call x2, Pallas kernels, exchange(): pl.pallas_call(functools.partial(exchange_kernel, groups, columns, with_l...  63 us
    dot_general x1, matrix products, local(): jnp.einsum('skr,kt->srt', stack, jnp.asarray(inverse_rows(devices)), pref...  10.2 us
    dot_general x1, matrix products, local(): lax.dot_general(forward, strain.reshape(windows * channels, NFFT), (((1,)...  9.7 us
    pallas_call x1, Pallas kernels, local(): pl.pallas_call(functools.partial(cross_kernel, groups, columns, entries,...  5.69 us
    convert_element_type x1, other arithmetic, local(): (spectrum * gain).astype(jnp.bfloat16)  2.92 us
    unnamed x3, local copies, waits for them, and re-layouts  2.36 us

profile of v1, /device:TPU:0, one launch (start us, length us, event | category | flops | bytes accessed | tf_op | source)
XLA Modules:
  0.0 98.8 jit_solution(11136592330456665257)
XLA Ops:
  0.0 0.0 copy-start
  0.0 1.6 %copy-done = bf16[2,128,4096]{2,1,0:T(8,128)(2,1)S(1)} copy-done((bf16[2,128,4096]{2,1,0:T(8,128)(2,1)S(1)}, bf16[2,128,4096]{2,1,0:T(8,128)(2,1)}, u32[]{:S(2)}) %copy-start) | copy-done | bytes 2097176
  1.6 0.7 convert_bitcast_fusion
  2.3 0.8 copy.18
  3.0 0.1 reshape.34
  3.1 0.7 pad_add_fusion
  3.9 0.6 broadcast_in_dim.10.refs_1_
  4.5 9.7 %multiply_reduce_fusion = (f32[32,256]{1,0:T(8,128)S(1)}, f32[32,2,32,256]{3,2,1,0:T(8,128)}) fusion(bf16[32,2,32,4096]{3,2,1,0:T(8,128)(2,1)} %constant.21, bf16[256,4096,1,1]{1,0,3,2:T(8,128)(2,1)S(1)} %bitcast.20), kind=kOutput, calls=%fused_computation.2 | convolution fusion | flops 4296007680 | bytes 21004288 | tf_op jit(solution)/shard_map/dot_general | solution.py:190
  14.3 2.9 %multiply_convert_fusion = bf16[32,2,32,256]{3,2,1,0:T(8,128)(2,1)} fusion(f32[32,2,32,256]{3,2,1,0:T(8,128)} %get-tuple-element.10, f32[32,256]{1,0:T(8,128)S(1)} %broadcast_in_dim.9), kind=kLoop, calls=%fused_computation.1 | loop fusion | flops 1048576 | bytes 3178496 | tf_op jit(solution)/shard_map/convert_element_type | solution.py:200
  17.2 32.8 %shard_map.64 = (bf16[32,64,256]{2,1,0:T(8,128)(2,1)}, s32[8,8,128]{2,1,0:T(8,128)}) custom-call(bf16[32,64,256]{2,1,0:T(8,128)(2,1)} %bitcast.21, s32[8,128]{1,0:T(8,128)} %broadcast_in_dim.10.refs_1_), custom_call_target="tpu_custom_call" | custom-call | tf_op jit(solution)/shard_map/pallas_call | solution.py:140
  50.0 0.8 copy.19
  50.8 0.6 slice_bitcast_fusion.lists_ref
  51.4 5.7 %shard_map.65.refs_0_ = bf16[32,2,64,128]{3,2,1,0:T(8,128)(2,1)} custom-call(s32[8,18]{1,0:T(8,128)} %slice_bitcast_fusion.lists_ref, bf16[32,64,256]{2,1,0:T(8,128)(2,1)} %get-tuple-element.8.rows_ref), custom_call_target="tpu_custom_call" | custom-call | tf_op jit(solution)/shard_map/pallas_call | solution.py:208
  57.1 30.2 %shard_map.66 = bf16[32,2,64,128]{3,2,1,0:T(8,128)(2,1)} custom-call(bf16[32,2,64,128]{3,2,1,0:T(8,128)(2,1)} %shard_map.65.refs_0_), custom_call_target="tpu_custom_call" | custom-call | tf_op jit(solution)/shard_map/pallas_call | solution.py:140
  87.3 1.3 %copy.20 = bf16[2,32,64,128]{3,2,1,0:T(8,128)(2,1)S(1)} copy(bf16[2,32,64,128]{3,2,0,1:T(8,128)(2,1)} %bitcast.22) | data formatting | bytes 2097152 | tf_op jit(solution)/shard_map/transpose | solution.py:216
  88.6 10.2 %convolution_bitcast_fusion = f32[1,1,2,128,4096]{4,3,2,1,0:T(8,128)} fusion(bf16[2,2048,128]{2,1,0:T(8,128)(2,1)S(1)} %bitcast.23, bf16[2048,4096,1]{1,0,2:T(8,128)(2,1)} %constant.22), kind=kOutput, calls=%fused_computation | convolution fusion | flops 4294967296 | bytes 22020096 | tf_op jit(solution)/shard_map/skr,kt->srt/dot_general | solution.py:217
  (6 shorter events, 0.1 us)
Async XLA Ops:
  0.0 1.6 %copy-start = (bf16[2,128,4096]{2,1,0:T(8,128)(2,1)S(1)}, bf16[2,128,4096]{2,1,0:T(8,128)(2,1)}, u32[]{:S(2)}) copy-start(bf16[2,128,4096]{2,1,0:T(8,128)(2,1)} %param.6) | copy-start | bytes 6291460

commit v2 on v0

v2 whole, which is shorter than its diff:
```python
import functools
import math

import jax
import jax.numpy as jnp
import numpy as np
from jax import lax
from jax.experimental import pallas as pl
from jax.experimental.pallas import tpu as pltpu
from jax.sharding import PartitionSpec as P

NFFT = 4096
NB = 1024
SUB = 64
BLK = 128
CAP = 2
LANES = 128
PHASES = 2
MESH = pl.DeviceIdType.MESH


def phases_of(devices):
    return max(1, min(PHASES, NB // devices // 8))


def table_rows(devices, samples, taper):
    phases = phases_of(devices)
    bins = (np.arange(NB, dtype=np.int64) + 1).reshape(phases, devices, 1, -1, 1)
    angles = np.mod(bins * samples, NFFT) * (2.0 * math.pi / NFFT)
    rows = np.concatenate([np.cos(angles), -np.sin(angles)], axis=2) * taper
    return rows.reshape(2 * NB, NFFT).astype(jnp.bfloat16)


@functools.lru_cache(maxsize=None)
def forward_rows(devices):
    samples = np.arange(NFFT, dtype=np.int64)
    taper = 0.5 - 0.5 * np.cos(samples * (2.0 * math.pi / NFFT))
    return table_rows(devices, samples, taper)


@functools.lru_cache(maxsize=None)
def inverse_rows(devices):
    return table_rows(devices, np.arange(NFFT, dtype=np.int64) - NFFT // 2, np.ones(NFFT))


def loop(low, high, body):
    def step_body(step, carry):
        body(step)
        return carry

    lax.fori_loop(low, high, step_body, 0)


def slot_row(groups, entries, pairs_ref, owners_ref):
    lane = lax.broadcasted_iota(jnp.int32, (8, LANES), 1)
    row = jnp.zeros((8, LANES), jnp.int32)
    for entry in range(entries):
        owner = owners_ref[0, entry]
        rank = jnp.int32(0)
        for before in range(entry):
            rank += (owners_ref[0, before] == owner).astype(jnp.int32)
        base = 3 * (owner * CAP + rank)
        row = jnp.where(lane == base, pairs_ref[0, 0, entry], row)
        row = jnp.where(lane == base + 1, pairs_ref[0, 1, entry], row)
        row = jnp.where(lane == base + 2, 1, row)
    return row


def correlate_kernel(
    groups, columns, phases, entries, windows, scale,
    pairs_ref, owners_ref, mask_ref, strain_ref, table_ref,
    stack_ref,
    table_buf, white_buf, list_buf, lists_buf, lists_smem, *rest,
):
    rows_bufs, slot_bufs = rest[:phases], rest[phases : 2 * phases]
    table_sem, own_sem, lsend_sem, lrecv_sem, wsend_sem, wrecv_sem, ssend_sem, srecv_sem = rest[
        2 * phases :
    ]
    devices = groups * columns
    my_group = lax.axis_index("grp")
    mine = lax.axis_index("ch")
    me = my_group * columns + mine
    tiles = phases * groups
    rows = white_buf.shape[2]
    half = rows // 2

    def tile_group(index):
        return lax.rem(index + my_group, groups)

    def tile_copy(index):
        place = lax.div(index, groups) * groups + tile_group(index)
        return pltpu.make_async_copy(
            table_ref.at[place], table_buf.at[index], table_sem.at[index]
        )

    loop(0, tiles, lambda index: tile_copy(index).start())

    barrier = pltpu.get_barrier_semaphore()

    def greet(step):
        to = lax.rem(me + step, devices)
        pl.semaphore_signal(
            barrier,
            inc=1,
            device_id=(lax.div(to, columns), lax.rem(to, columns)),
            device_id_type=MESH,
        )

    loop(1, devices, greet)
    list_buf[...] = slot_row(groups, entries, pairs_ref, owners_ref)

    def compute_tile(index):
        tile_copy(index).wait()
        spectrum = lax.dot_general(
            table_buf[index],
            strain_ref[...],
            (((1,), (1,)), ((), ())),
            preferred_element_type=jnp.float32,
        )
        lanes = spectrum.shape[1]
        parts = spectrum.reshape(columns, 2, half, lanes)
        power = parts[:, 0] * parts[:, 0] + parts[:, 1] * parts[:, 1]
        bands = columns * half // SUB
        band_power = jnp.sum(power.reshape(bands, SUB, lanes), axis=1, keepdims=True) / SUB
        usable = jnp.concatenate([mask_ref[w : w + 1, :] for w in range(windows)], axis=1)
        gain = usable.astype(jnp.float32).reshape(1, 1, lanes) / jnp.sqrt(band_power + 1e-06)
        gain = jnp.broadcast_to(gain, (bands, SUB, lanes)).reshape(columns, 1, half, lanes)
        white_buf[index] = (parts * gain).reshape(columns, rows, lanes).astype(jnp.bfloat16)

    def white_copy(phase, index, column):
        to_group = tile_group(index)
        to = to_group * columns + column
        return pltpu.make_async_remote_copy(
            src_ref=white_buf.at[index, column],
            dst_ref=rows_bufs[phase].at[me],
            send_sem=wsend_sem.at[phase, to],
            recv_sem=wrecv_sem.at[phase, me],
            device_id=(to_group, column),
            device_id_type=MESH,
        )

    def white_own(phase, index):
        return pltpu.make_async_copy(
            white_buf.at[index, mine], rows_bufs[phase].at[me], wrecv_sem.at[phase, me]
        )

    def send_tile(phase, index):
        def send(step):
            column = lax.rem(mine + step, columns)
            away = (tile_group(index) != my_group) | (column != mine)

            @pl.when(away)
            def _():
                white_copy(phase, index, column).start()

            @pl.when(jnp.logical_not(away))
            def _():
                white_own(phase, index).start()

        loop(0, columns, send)

    def list_copy(step):
        return pltpu.make_async_remote_copy(
            src_ref=list_buf,
            dst_ref=lists_buf.at[mine],
            send_sem=lsend_sem.at[step],
            recv_sem=lrecv_sem.at[step],
            device_id=(my_group, lax.rem(mine + step, columns)),
            device_id_type=MESH,
        )

    compute_tile(0)
    pl.semaphore_wait(barrier, devices - 1)
    loop(1, columns, lambda step: list_copy(step).start())
    own_list = pltpu.make_async_copy(list_buf, lists_buf.at[mine], own_sem.at[0])
    own_list.start()
    for phase in range(phases):

        def compute_and_send(index, phase=phase):
            compute_tile(index)
            send_tile(phase, index - 1)

        loop(phase * groups + 1, (phase + 1) * groups, compute_and_send)
        if phase + 1 < phases:
            compute_tile((phase + 1) * groups)
        send_tile(phase, (phase + 1) * groups - 1)

    own_list.wait()
    loop(1, columns, lambda step: list_copy(step).wait())
    to_smem = pltpu.make_async_copy(lists_buf, lists_smem, own_sem.at[1])
    to_smem.start()
    to_smem.wait()

    def slot_copy(phase, group, column):
        return pltpu.make_async_remote_copy(
            src_ref=slot_bufs[phase].at[group, column],
            dst_ref=stack_ref.at[:, phase, me],
            send_sem=ssend_sem.at[phase, group * columns + column],
            recv_sem=srecv_sem.at[phase, me],
            device_id=(group, column),
            device_id_type=MESH,
        )

    def slot_own(phase):
        return pltpu.make_async_copy(
            slot_bufs[phase].at[my_group, mine], stack_ref.at[:, phase, me], srecv_sem.at[phase, me]
        )

    def cross_column(phase, column):
        rows_ref = rows_bufs[phase]
        for owner in range(groups):
            for rank in range(CAP):
                base = 3 * (owner * CAP + rank)
                first = lists_smem[column, 0, base]
                second = lists_smem[column, 0, base + 1]
                factor = lists_smem[column, 0, base + 2].astype(jnp.float32) * scale
                real = jnp.zeros((half, BLK), jnp.float32)
                imag = jnp.zeros((half, BLK), jnp.float32)
                for group in range(groups):
                    a = rows_ref[group * columns + first].astype(jnp.float32)
                    b = rows_ref[group * columns + second].astype(jnp.float32)
                    for window in range(windows):
                        lanes = slice(window * BLK, (window + 1) * BLK)
                        a_real, a_imag = a[:half, lanes], a[half:, lanes]
                        b_real, b_imag = b[:half, lanes], b[half:, lanes]
                        real += a_real * b_real + a_imag * b_imag
                        imag += a_real * b_imag - a_imag * b_real
                both = jnp.concatenate([real, imag], axis=0) * factor
                slot_bufs[phase][owner, column, rank] = both.astype(jnp.bfloat16)

    def send_column(phase, column):
        def send(step):
            group = lax.rem(my_group + step, groups)
            away = (group != my_group) | (column != mine)

            @pl.when(away)
            def _():
                slot_copy(phase, group, column).start()

            @pl.when(jnp.logical_not(away))
            def _():
                slot_own(phase).start()

        loop(0, groups, send)

    def wait_from(phase, sem, part):
        def wait(source):
            @pl.when(source != me)
            def _():
                pltpu.make_async_remote_copy(
                    src_ref=part(source),
                    dst_ref=part(source),
                    send_sem=sem.at[phase, source],
                    recv_sem=sem.at[phase, source],
                    device_id=(lax.div(source, columns), lax.rem(source, columns)),
                    device_id_type=MESH,
                ).wait_recv()

        loop(0, devices, wait)

    for phase in range(phases):
        white_own(phase, phase * groups).wait()
        wait_from(phase, wrecv_sem, lambda source: rows_bufs[phase].at[source])

        cross_column(phase, mine)

        def cross_and_send(step, phase=phase):
            cross_column(phase, lax.rem(mine + step, columns))
            send_column(phase, lax.rem(mine + step - 1, columns))

        loop(1, columns, cross_and_send)
        send_column(phase, lax.rem(mine + columns - 1, columns))

    for phase in range(phases):
        slot_own(phase).wait()
        wait_from(phase, srecv_sem, lambda source: stack_ref.at[:, phase, source])

        def wait_sends(to, phase=phase):
            group, column = lax.div(to, columns), lax.rem(to, columns)

            @pl.when(to != me)
            def _():
                index = phase * groups + lax.rem(group - my_group + groups, groups)
                white_copy(phase, index, column).wait_send()
                slot_copy(phase, group, column).wait_send()

        loop(0, devices, wait_sends)


def local(strain, valid_mask, pair_list, owner_group):
    windows, channels = valid_mask.shape
    groups = lax.axis_size("grp")
    columns = lax.axis_size("ch")
    devices = groups * columns
    entries = owner_group.shape[1]
    phases = phases_of(devices)
    rows = 2 * NB // devices // phases
    lanes = windows * channels
    tiles = phases * groups
    scale = 1.0 / math.sqrt(NB * windows * groups)

    vmem = pl.BlockSpec(memory_space=pltpu.VMEM)
    smem = pl.BlockSpec(memory_space=pltpu.SMEM)
    dma = pltpu.SemaphoreType.DMA
    stack = pl.pallas_call(
        functools.partial(correlate_kernel, groups, columns, phases, entries, windows, scale),
        out_shape=jax.ShapeDtypeStruct((CAP, phases, devices, rows, BLK), jnp.bfloat16),
        in_specs=[smem, smem, vmem, vmem, pl.BlockSpec(memory_space=pl.ANY)],
        out_specs=vmem,
        scratch_shapes=[
            pltpu.VMEM((tiles, columns * rows, NFFT), jnp.bfloat16),
            pltpu.VMEM((tiles, columns, rows, lanes), jnp.bfloat16),
            pltpu.VMEM((8, LANES), jnp.int32),
            pltpu.VMEM((columns, 8, LANES), jnp.int32),
            pltpu.SMEM((columns, 8, LANES), jnp.int32),
        ]
        + [pltpu.VMEM((devices, rows, lanes), jnp.bfloat16) for _ in range(phases)]
        + [pltpu.VMEM((groups, columns, CAP, rows, BLK), jnp.bfloat16) for _ in range(phases)]
        + [dma((tiles,)), dma((2,)), dma((columns,)), dma((columns,))]
        + [dma((phases, devices)) for _ in range(4)],
        compiler_params=pltpu.CompilerParams(
            collective_id=0, has_side_effects=True, vmem_limit_bytes=48 * 1024 * 1024
        ),
    )(
        pair_list.transpose(0, 2, 1),
        owner_group,
        valid_mask,
        strain.reshape(lanes, NFFT),
        jnp.asarray(forward_rows(devices)).reshape(tiles, columns * rows, NFFT),
    )
    stacked = jnp.einsum(
        "skr,kt->srt",
        stack.reshape(CAP, 2 * NB, BLK),
        jnp.asarray(inverse_rows(devices)),
        preferred_element_type=jnp.float32,
    )
    return stacked.reshape(1, 1, CAP, BLK, NFFT)


def solution(mesh):
    placed = (P("grp", "ch", None), P("grp", "ch"), P("ch", None, None), P("ch", None))
    return jax.shard_map(
        local,
        mesh=mesh,
        in_specs=placed,
        out_specs=P("grp", "ch", None, None, None),
        check_vma=False,
    )
```

time: 476 us -> 70.2 us (0.15)
  waiting for transfers between devices: 210 us -> 0 us
  other arithmetic: 162 us -> 0 us
  Pallas kernels: 0 us -> 55.1 us
  matrix products: 51.5 us -> 10.2 us
  local copies, waits for them, and re-layouts: 30.2 us -> 3.6 us
  between operations: 13.5 us -> 0.01 us
  loops' own time: 7.78 us -> 0 us
    all_gather x1 -> x0, waiting for transfers between devices: 128 us -> none  [local(): gathered = lax.all_gather(white, 'ch', axis=1, tiled=True)]
    psum x1 -> x0, waiting for transfers between devices: 82.5 us -> none  [local(): summed = lax.psum(flat_partial, 'grp')]
    another operation x1 -> x0, other arithmetic: 69.9 us -> none
    cos x1 -> x0, other arithmetic: 68.4 us -> none  [inverse_table(): return jnp.concatenate([jnp.cos(angles), -jnp.sin(angles)], axis=0)]
    pallas_call x0 -> x1, Pallas kernels: none -> 55.1 us  [local(): pl.pallas_call(functools.partial(correlate_kernel, groups, columns, phase...]
    dot_general x3 -> x1, matrix products: 51.5 us -> 10.2 us  [local(): jnp.einsum('skr,kt->srt', stack.reshape(CAP, 2 * NB, BLK), jnp.asarray(in...]
    convert_element_type x8 -> x0, other arithmetic: 13.3 us -> none  [the longest x6 11.3 us: cross_block(): lax.dynamic_slice_in_dim(rows, pair_entry[0] * block, block, 1)]
    while x1 -> x0, local copies, waits for them, and re-layouts: 11.7 us -> none  [local(): lax.map(lambda pair_entry: cross_block(gathered, pair_entry, BLK, NB), pa...]
  transfers between devices with their start and end apart: 2 -> 0, of which waited for: 2 -> 0; matrix products, arithmetic and copies ran while one was open for 14% -> 0% of each run, Pallas kernels for 0% -> 0%
where the time goes in v2:
time: 70.2 us; the launch traced here: 68.9 us
  Pallas kernels  55.1 us (78%)
  matrix products  10.2 us (15%)
  local copies, waits for them, and re-layouts  3.6 us (5%)
    pallas_call x1, Pallas kernels, local(): pl.pallas_call(functools.partial(correlate_kernel, groups, columns, phase...  55.1 us
    dot_general x1, matrix products, local(): jnp.einsum('skr,kt->srt', stack.reshape(CAP, 2 * NB, BLK), jnp.asarray(in...  10.2 us
    unnamed x8, local copies, waits for them, and re-layouts  3.6 us

profile of v2, /device:TPU:0, one launch (start us, length us, event | category | flops | bytes accessed | tf_op | source)
XLA Modules:
  0.0 68.9 jit_solution(3939248439491479862)
XLA Ops:
  0.0 0.0 copy-start
  0.0 1.6 %copy-done = bf16[2,128,4096]{2,1,0:T(8,128)(2,1)S(1)} copy-done((bf16[2,128,4096]{2,1,0:T(8,128)(2,1)S(1)}, bf16[2,128,4096]{2,1,0:T(8,128)(2,1)}, u32[]{:S(2)}) %copy-start) | copy-done | bytes 2097176
  1.6 0.0 copy-start.1
  1.6 0.7 copy-done.1
  2.3 0.0 copy-start.2
  2.3 0.7 copy-done.2
  3.0 0.0 copy-start.3
  3.0 0.7 copy-done.3
  3.6 55.1 %shard_map.64 = bf16[2,2,32,32,128]{4,3,2,1,0:T(8,128)(2,1)S(1)} custom-call(s32[1,2,6]{2,1,0:T(2,128)S(1)} %bitcast.10, s32[1,6]{1,0:T(1,128)S(1)} %copy-done.3, s32[2,128]{1,0:T(2,128)S(1)} %copy-done.2, bf16[256,4096]{1,0:T(8,128)(2,1)S(1)} %bitcast.9, bf16[8,256,4096]{2,1,0:T(8,128)(2,1)} %constant.10.table_ref), custom_call_target="tpu_custom_call" | custom-call | tf_op jit(solution)/shard_map/pallas_call | solution.py:305
  58.7 10.2 %convolution_bitcast_fusion = f32[1,1,2,128,4096]{4,3,2,1,0:T(8,128)} fusion(bf16[2,2048,128]{2,1,0:T(8,128)(2,1)S(1)} %bitcast.8, bf16[2048,4096,1]{1,0,2:T(8,128)(2,1)} %constant.11), kind=kOutput, calls=%fused_computation | convolution fusion | flops 4294967296 | bytes 22020096 | tf_op jit(solution)/shard_map/skr,kt->srt/dot_general | solution.py:331
Async XLA Ops:
  0.0 1.6 %copy-start = (bf16[2,128,4096]{2,1,0:T(8,128)(2,1)S(1)}, bf16[2,128,4096]{2,1,0:T(8,128)(2,1)}, u32[]{:S(2)}) copy-start(bf16[2,128,4096]{2,1,0:T(8,128)(2,1)} %param.6) | copy-start | bytes 6291460
  1.6 0.7 copy-start.1
  2.3 0.7 copy-start.2
  3.0 0.7 copy-start.3

commit v3 on v2

--- a/solution.py
+++ b/solution.py
@@ -16,6 +16,7 @@
 CAP = 2
 LANES = 128
 PHASES = 2
+LAGS = 512
 MESH = pl.DeviceIdType.MESH
 
 
@@ -68,13 +69,19 @@
 
 def correlate_kernel(
     groups, columns, phases, entries, windows, scale,
-    pairs_ref, owners_ref, mask_ref, strain_ref, table_ref,
-    stack_ref,
-    table_buf, white_buf, list_buf, lists_buf, lists_smem, *rest,
+    pairs_hbm, owners_hbm, mask_hbm, strain_hbm, table_ref, inverse_ref, *rest,
 ):
+    outs = 2 if phases > 1 else 1
+    last_stack, total_hbm = rest[0], rest[outs - 1]
+    pairs_ref, owners_ref, mask_ref, strain_ref, inverse_buf, left_buf = rest[outs : outs + 6]
+    table_buf, white_buf, list_buf, lists_buf, lists_smem = rest[outs + 6 : outs + 11]
+    total_ref, total_sem = rest[outs + 11 : outs + 13]
+    rest = rest[outs + 13 :]
     rows_bufs, slot_bufs = rest[:phases], rest[phases : 2 * phases]
+    stack_bufs = list(rest[2 * phases : 3 * phases - 1]) + [last_stack]
+    in_sem, inverse_sem = rest[3 * phases - 1 : 3 * phases + 1]
     table_sem, own_sem, lsend_sem, lrecv_sem, wsend_sem, wrecv_sem, ssend_sem, srecv_sem = rest[
-        2 * phases :
+        3 * phases + 1 :
     ]
     devices = groups * columns
     my_group = lax.axis_index("grp")
@@ -93,7 +100,28 @@
             table_ref.at[place], table_buf.at[index], table_sem.at[index]
         )
 
+    inputs = [
+        pltpu.make_async_copy(source, target, in_sem.at[place])
+        for place, (source, target) in enumerate(
+            [
+                (pairs_hbm, pairs_ref),
+                (owners_hbm, owners_ref),
+                (mask_hbm, mask_ref),
+                (strain_hbm, strain_ref),
+            ]
+        )
+    ]
+    for copy in inputs:
+        copy.start()
     loop(0, tiles, lambda index: tile_copy(index).start())
+
+    def inverse_copy(phase):
+        return pltpu.make_async_copy(
+            inverse_ref.at[phase], inverse_buf.at[phase], inverse_sem.at[phase]
+        )
+
+    for phase in range(phases - 1):
+        inverse_copy(phase).start()
 
     barrier = pltpu.get_barrier_semaphore()
 
@@ -107,6 +135,8 @@
         )
 
     loop(1, devices, greet)
+    for copy in inputs:
+        copy.wait()
     list_buf[...] = slot_row(groups, entries, pairs_ref, owners_ref)
 
     def compute_tile(index):
@@ -194,7 +224,7 @@
     def slot_copy(phase, group, column):
         return pltpu.make_async_remote_copy(
             src_ref=slot_bufs[phase].at[group, column],
-            dst_ref=stack_ref.at[:, phase, me],
+            dst_ref=stack_bufs[phase].at[:, me],
             send_sem=ssend_sem.at[phase, group * columns + column],
             recv_sem=srecv_sem.at[phase, me],
             device_id=(group, column),
@@ -203,7 +233,7 @@
 
     def slot_own(phase):
         return pltpu.make_async_copy(
-            slot_bufs[phase].at[my_group, mine], stack_ref.at[:, phase, me], srecv_sem.at[phase, me]
+            slot_bufs[phase].at[my_group, mine], stack_bufs[phase].at[:, me], srecv_sem.at[phase, me]
         )
 
     def cross_column(phase, column):
@@ -273,7 +303,26 @@
 
     for phase in range(phases):
         slot_own(phase).wait()
-        wait_from(phase, srecv_sem, lambda source: stack_ref.at[:, phase, source])
+        wait_from(phase, srecv_sem, lambda source: stack_bufs[phase].at[:, source])
+        if phase < phases - 1:
+            inverse_copy(phase).wait()
+            depth = devices * rows
+            for rank in range(CAP):
+                block = stack_bufs[phase][rank].reshape(depth, BLK).astype(jnp.float32)
+                left_buf[rank * BLK : (rank + 1) * BLK, :] = block.T.astype(jnp.bfloat16)
+
+            def inverse_tile(tile, phase=phase):
+                at = pl.ds(pl.multiple_of(tile * LAGS, LAGS), LAGS)
+                part = jnp.dot(
+                    left_buf[...], inverse_buf[phase, :, at], preferred_element_type=jnp.float32
+                )
+                total_ref[:, at] = part if phase == 0 else total_ref[:, at] + part
+
+            loop(0, NFFT // LAGS, inverse_tile)
+        if phase == phases - 2:
+            total_copy = pltpu.make_async_copy(total_ref, total_hbm, total_sem.at[0])
+            total_copy.start()
+
 
         def wait_sends(to, phase=phase):
             group, column = lax.div(to, columns), lax.rem(to, columns)
@@ -285,6 +334,8 @@
                 slot_copy(phase, group, column).wait_send()
 
         loop(0, devices, wait_sends)
+    if phases > 1:
+        total_copy.wait()
 
 
 def local(strain, valid_mask, pair_list, owner_group):
@@ -300,26 +351,42 @@
     scale = 1.0 / math.sqrt(NB * windows * groups)
 
     vmem = pl.BlockSpec(memory_space=pltpu.VMEM)
-    smem = pl.BlockSpec(memory_space=pltpu.SMEM)
     dma = pltpu.SemaphoreType.DMA
-    stack = pl.pallas_call(
+    anywhere = pl.BlockSpec(memory_space=pltpu.HBM)
+    stack_shape = (CAP, devices, rows, BLK)
+    depth = devices * rows
+    outs = [jax.ShapeDtypeStruct(stack_shape, jnp.bfloat16)]
+    if phases > 1:
+        outs.append(jax.ShapeDtypeStruct((CAP * BLK, NFFT), jnp.float32))
+    inverse = inverse_rows(devices).reshape(phases, depth, NFFT)
+    stack, *total = pl.pallas_call(
         functools.partial(correlate_kernel, groups, columns, phases, entries, windows, scale),
-        out_shape=jax.ShapeDtypeStruct((CAP, phases, devices, rows, BLK), jnp.bfloat16),
-        in_specs=[smem, smem, vmem, vmem, pl.BlockSpec(memory_space=pl.ANY)],
-        out_specs=vmem,
+        out_shape=outs,
+        in_specs=[anywhere] * 6,
+        out_specs=[vmem, anywhere][: len(outs)],
         scratch_shapes=[
+            pltpu.SMEM((1, 2, entries), jnp.int32),
+            pltpu.SMEM((1, entries), jnp.int32),
+            pltpu.VMEM((windows, channels), jnp.int32),
+            pltpu.VMEM((lanes, NFFT), jnp.bfloat16),
+            pltpu.VMEM((max(1, phases - 1), depth if phases > 1 else 16, NFFT), jnp.bfloat16),
+            pltpu.VMEM((CAP * BLK, depth), jnp.bfloat16),
             pltpu.VMEM((tiles, columns * rows, NFFT), jnp.bfloat16),
             pltpu.VMEM((tiles, columns, rows, lanes), jnp.bfloat16),
             pltpu.VMEM((8, LANES), jnp.int32),
             pltpu.VMEM((columns, 8, LANES), jnp.int32),
             pltpu.SMEM((columns, 8, LANES), jnp.int32),
+            pltpu.VMEM((CAP * BLK, NFFT if phases > 1 else LANES), jnp.float32),
+            dma((1,)),
         ]
         + [pltpu.VMEM((devices, rows, lanes), jnp.bfloat16) for _ in range(phases)]
         + [pltpu.VMEM((groups, columns, CAP, rows, BLK), jnp.bfloat16) for _ in range(phases)]
+        + [pltpu.VMEM(stack_shape, jnp.bfloat16) for _ in range(phases - 1)]
+        + [dma((4,)), dma((phases,))]
         + [dma((tiles,)), dma((2,)), dma((columns,)), dma((columns,))]
         + [dma((phases, devices)) for _ in range(4)],
         compiler_params=pltpu.CompilerParams(
-            collective_id=0, has_side_effects=True, vmem_limit_bytes=48 * 1024 * 1024
+            collective_id=0, has_side_effects=True, vmem_limit_bytes=52 * 1024 * 1024
         ),
     )(
         pair_list.transpose(0, 2, 1),
@@ -327,13 +394,16 @@
         valid_mask,
         strain.reshape(lanes, NFFT),
         jnp.asarray(forward_rows(devices)).reshape(tiles, columns * rows, NFFT),
+        jnp.asarray(inverse[: max(1, phases - 1)]),
     )
     stacked = jnp.einsum(
         "skr,kt->srt",
-        stack.reshape(CAP, 2 * NB, BLK),
-        jnp.asarray(inverse_rows(devices)),
+        stack.reshape(CAP, depth, BLK),
+        jnp.asarray(inverse[phases - 1]),
         preferred_element_type=jnp.float32,
     )
+    if phases > 1:
+        stacked = stacked + total[0].reshape(CAP, BLK, NFFT)
     return stacked.reshape(1, 1, CAP, BLK, NFFT)
 
 

time: 70.2 us -> 65.1 us (0.927)
  matrix products: 10.2 us -> 6.61 us
  local copies, waits for them, and re-layouts: 3.6 us -> 2.02 us
    dot_general x1, matrix products: 10.2 us -> 6.61 us  [local(): jnp.einsum('skr,kt->srt', stack.reshape(CAP, depth, BLK), jnp.asarray(inv...]
    unnamed x8, local copies, waits for them, and re-layouts: 3.6 us -> 2.02 us
where the time goes in v3:
time: 65.1 us; the launch traced here: 64 us
  Pallas kernels  55.4 us (85%)
  matrix products  6.61 us (10%)
  local copies, waits for them, and re-layouts  2.02 us (3%)
    pallas_call x1, Pallas kernels, local(): pl.pallas_call(functools.partial(correlate_kernel, groups, columns, phase...  55.4 us
    dot_general x1, matrix products, local(): jnp.einsum('skr,kt->srt', stack.reshape(CAP, depth, BLK), jnp.asarray(inv...  6.61 us
    unnamed x8, local copies, waits for them, and re-layouts  2.02 us

profile of v3, /device:TPU:0, one launch (start us, length us, event | category | flops | bytes accessed | tf_op | source)
XLA Modules:
  0.0 64.0 jit_solution(7030938733292065271)
XLA Ops:
  0.0 0.0 copy-start
  0.0 0.7 %copy-done = s32[1,6,2]{1,2,0:T(2,128)S(1)} copy-done((s32[1,6,2]{1,2,0:T(2,128)S(1)}, s32[1,6,2]{1,2,0:T(2,128)}, u32[]{:S(2)}) %copy-start) | copy-done | bytes 72
  0.7 0.0 copy-start.1
  0.7 0.7 %copy-done.1 = s32[2,128]{1,0:T(2,128)S(1)} copy-done((s32[2,128]{1,0:T(2,128)S(1)}, s32[2,128]{1,0:T(2,128)}, u32[]{:S(2)}) %copy-start.1) | copy-done | bytes 1048
  1.4 0.0 copy-start.2
  1.4 0.7 %copy-done.2 = s32[1,6]{1,0:T(1,128)S(1)} copy-done((s32[1,6]{1,0:T(1,128)S(1)}, s32[1,6]{1,0:T(1,128)}, u32[]{:S(2)}) %copy-start.2) | copy-done | bytes 48
  2.0 0.0 copy-start.3
  2.0 55.4 %shard_map.73 = (bf16[2,32,32,128]{3,2,1,0:T(8,128)(2,1)S(1)}, f32[256,4096]{1,0:T(8,128)}) custom-call(s32[1,2,6]{2,1,0:T(2,128)S(1)} %bitcast.10, s32[1,6]{1,0:T(1,128)S(1)} %copy-done.2, s32[2,128]{1,0:T(2,128)S(1)} %copy-done.1, bf16[256,4096]{1,0:T(8,128)(2,1)} %bitcast.12, bf16[8,256,4096]{2,1,0:T(8,128)(2,1)} %constant.13.table_ref, ...), custom_call_target="tpu_custom_call" | custom-call | tf_op jit(solution)/shard_map/pallas_call | solution.py:362
  57.4 0.0 copy-done.3
  57.4 6.6 %fusion = f32[1,1,2,128,4096]{4,3,2,1,0:T(8,128)} fusion(f32[2,128,4096]{2,1,0:T(8,128)} %bitcast.11, bf16[2,1024,128]{2,1,0:T(8,128)(2,1)S(1)} %bitcast.9, bf16[1024,4096,1]{1,0,2:T(8,128)(2,1)S(1)} %copy-done.3), kind=kOutput, calls=%fused_computation.1 | convolution fusion | flops 2148532224 | bytes 17301504 | tf_op jit(solution)/shard_map/skr,kt->srt/dot_general | solution.py:399
Async XLA Ops:
  0.0 0.7 %copy-start = (s32[1,6,2]{1,2,0:T(2,128)S(1)}, s32[1,6,2]{1,2,0:T(2,128)}, u32[]{:S(2)}) copy-start(s32[1,6,2]{1,2,0:T(2,128)} %param.9) | copy-start | bytes 148
  0.7 0.7 %copy-start.1 = (s32[2,128]{1,0:T(2,128)S(1)}, s32[2,128]{1,0:T(2,128)}, u32[]{:S(2)}) copy-start(s32[2,128]{1,0:T(2,128)} %mask_hbm.1) | copy-start | bytes 3076
  1.4 0.7 %copy-start.2 = (s32[1,6]{1,0:T(1,128)S(1)}, s32[1,6]{1,0:T(1,128)}, u32[]{:S(2)}) copy-start(s32[1,6]{1,0:T(1,128)} %owners_hbm.1) | copy-start | bytes 76
  2.0 55.4 %copy-start.3 = (bf16[1024,4096,1]{1,0,2:T(8,128)(2,1)S(1)}, bf16[1024,4096,1]{1,0,2:T(8,128)(2,1)}, u32[]{:S(2)}) copy-start(bf16[1024,4096,1]{1,0,2:T(8,128)(2,1)} %constant.14) | copy-start | bytes 25165828

commit v4 on v3

--- a/solution.py
+++ b/solution.py
@@ -15,7 +15,7 @@
 BLK = 128
 CAP = 2
 LANES = 128
-PHASES = 2
+PHASES = 4
 LAGS = 512
 MESH = pl.DeviceIdType.MESH
 

time: 65.1 us -> 69.2 us (1.063); the launches traced: 64 us -> 69 us
  Pallas kernels: 55.4 us -> 61.4 us
  matrix products: 6.61 us -> 5.6 us
    pallas_call x1, Pallas kernels: 55.4 us -> 61.4 us  [local(): pl.pallas_call(functools.partial(correlate_kernel, groups, columns, phase...]
    dot_general x1, matrix products: 6.61 us -> 5.6 us  [local(): jnp.einsum('skr,kt->srt', stack.reshape(CAP, depth, BLK), jnp.asarray(inv...]
where the time goes in v4:
time: 69.2 us; the launch traced here: 69 us
  Pallas kernels  61.4 us (89%)
  matrix products  5.6 us (8%)
  local copies, waits for them, and re-layouts  2.02 us (3%)
    pallas_call x1, Pallas kernels, local(): pl.pallas_call(functools.partial(correlate_kernel, groups, columns, phase...  61.4 us
    dot_general x1, matrix products, local(): jnp.einsum('skr,kt->srt', stack.reshape(CAP, depth, BLK), jnp.asarray(inv...  5.6 us
    unnamed x8, local copies, waits for them, and re-layouts  2.02 us

profile of v4, /device:TPU:0, one launch (start us, length us, event | category | flops | bytes accessed | tf_op | source)
XLA Modules:
  0.0 69.0 jit_solution(14306582827502187251)
XLA Ops:
  0.0 0.0 copy-start
  0.0 0.7 copy-done
  0.7 0.0 copy-start.1
  0.7 0.7 copy-done.1
  1.4 0.0 copy-start.2
  1.4 0.7 copy-done.2
  2.0 0.0 copy-start.3
  2.0 61.4 %shard_map.73 = (bf16[2,32,16,128]{3,2,1,0:T(8,128)(2,1)S(1)}, f32[256,4096]{1,0:T(8,128)}) custom-call(s32[1,2,6]{2,1,0:T(2,128)S(1)} %bitcast.10, s32[1,6]{1,0:T(1,128)S(1)} %copy-done.2, s32[2,128]{1,0:T(2,128)S(1)} %copy-done.1, bf16[256,4096]{1,0:T(8,128)(2,1)} %bitcast.12, bf16[16,128,4096]{2,1,0:T(8,128)(2,1)} %constant.13.table_ref, ...), custom_call_target="tpu_custom_call" | custom-call | tf_op jit(solution)/shard_map/pallas_call | solution.py:362
  63.4 0.0 copy-done.3
  63.4 5.6 %fusion = f32[1,1,2,128,4096]{4,3,2,1,0:T(8,128)} fusion(f32[2,128,4096]{2,1,0:T(8,128)} %bitcast.11, bf16[2,512,128]{2,1,0:T(8,128)(2,1)S(1)} %bitcast.9, bf16[512,4096,1]{1,0,2:T(8,128)(2,1)S(1)} %copy-done.3), kind=kOutput, calls=%fused_computation.1 | convolution fusion | flops 1074790400 | bytes 12845056 | tf_op jit(solution)/shard_map/skr,kt->srt/dot_general | solution.py:399
Async XLA Ops:
  0.0 0.7 copy-start
  0.7 0.7 copy-start.1
  1.4 0.7 copy-start.2
  2.0 61.4 %copy-start.3 = (bf16[512,4096,1]{1,0,2:T(8,128)(2,1)S(1)}, bf16[512,4096,1]{1,0,2:T(8,128)(2,1)}, u32[]{:S(2)}) copy-start(bf16[512,4096,1]{1,0,2:T(8,128)(2,1)} %constant.14) | copy-start | bytes 12582916
